TPU v7x, 32 devices: a whole 2x2x4 slice. The times are simulated.
32 devices in a mesh: row: 4 (over y, core), blk: 8 (over z, x).
Axes of the slice: x: 2, y: 2, z: 4, core: 2. Of those that a mesh axis runs over, the one named last changes fastest.
Arguments:
- right_side: float32 [4, 8, 8, 32, 256], P('row', 'blk')
- noise_level: float32 [4, 8, 8, 256], P('row', 'blk'), may hold values from 3 to 6
- near_blocks: bfloat16 [4, 8, 8, 9, 256, 256], P('row', 'blk'), as said below
- skeleton_basis: bfloat16 [4, 8, 8, 64, 256], P('row', 'blk'), may hold values from -0.125 to 0.125
- skeleton_index: int32 [4, 8, 64], P('row', 'blk'), may hold values from 0 to 2047, as said below
- far_list: int32 [4, 8, 7], P('row', 'blk'), may hold values from 0 to 7, as said below
- couplings: bfloat16 [4, 8, 7, 64, 64], P('row', 'blk'), as said below
Outputs:
- solution: float32 [4, 8, 8, 32, 256], P('row', 'blk')
- residual: float32 [4, 8, 8, 32, 256], P('row', 'blk')
- quadratic: float32 [32], replicated
Inputs may be any that keep to these rules, and one draw needn't show every extreme that they name: `far_list`: each device's 7 entries are distinct, none is the device's own blk index, and the two cyclic neighbours along blk are always among them; box b lists box b' exactly when b' lists b, and within a row every box's far boxes lie at the same set of cyclic offsets from its own index. `couplings`: the coupling that box b holds for far box b' is the transpose of the one that b' holds for b. `near_blocks`: A leaf's block for near slot s is the transpose of the block that its slot-s neighbour holds for slot 8 - s; slot 4 blocks are symmetric. `skeleton_index`: each device's 64 entries are distinct tracers of its 2048.
All inputs are finite; a program needn't handle non-finite values.
Results may differ from a plain program's by a relative error of at most 0.03.
Values may be sent and summed in bfloat16 or wider, within the bound.
A program may use at most 64 MiB of HBM per device.

v0:
```python
import jax
import jax.numpy as jnp
from jax import lax
from jax.sharding import PartitionSpec as P

ITERS = 4
LEAF_ROWS = 2
LEAF_COLS = 4


def extended_2(array, sides, width):
    for axis, dim in sides:
        count, length = (lax.axis_size(axis), array.shape[dim])
        up = [(i, (i + 1) % count) for i in range(count)]
        down = [(j, i) for i, j in up]
        last = lax.slice_in_dim(array, length - width, length, axis=dim)
        leading = lax.slice_in_dim(array, 0, width, axis=dim)
        before = lax.ppermute(last, axis, up)
        after = lax.ppermute(leading, axis, down)
        array = jnp.concatenate([before, array, after], axis=dim)
    return array


def local(
    right_side, noise_level, near_blocks, skeleton_basis, skeleton_index, far_list, couplings
):
    local_noise = noise_level[0, 0][:, None, :]
    leaf_count = near_blocks.shape[2]
    width = near_blocks.shape[4]
    blocks_grid = near_blocks[0, 0].reshape(LEAF_ROWS, LEAF_COLS, 9, width, width)
    basis_local = skeleton_basis[0, 0]
    skeleton_local = skeleton_index[0, 0]
    far_local = far_list[0, 0]
    coupling_local = couplings[0, 0]
    points = basis_local.shape[2]
    owner_leaf = skeleton_local // points
    owner_point = skeleton_local % points

    def column_sum(values):
        return jnp.sum(values, axis=(0, 1, 2, 4))

    def residual_sum(values):
        return lax.psum(column_sum(values * values), ("row", "blk"))

    solution = jnp.zeros_like(right_side)
    residual = right_side
    direction = right_side
    norm_now = residual_sum(residual)
    for step_index in range(ITERS):
        rounded = direction.astype(jnp.bfloat16)
        own_field = rounded[0, 0]
        columns = own_field.shape[1]
        leaf_grid = own_field.reshape(LEAF_ROWS, LEAF_COLS, columns, width)
        extended = extended_2(leaf_grid, (("row", 0), ("blk", 1)), 1)
        sources = jnp.stack(
            [
                extended[slot // 3 : slot // 3 + LEAF_ROWS, slot % 3 : slot % 3 + LEAF_COLS]
                for slot in range(9)
            ],
            axis=2,
        )
        near = jnp.einsum(
            "abkci,abkij->abcj", sources, blocks_grid, preferred_element_type=jnp.float32
        )
        result = near.reshape(leaf_count, columns, width)
        picked = own_field[owner_leaf, :, owner_point].astype(jnp.float32)
        skeleton = picked.T + jnp.einsum(
            "lci,lki->ck", own_field, basis_local, preferred_element_type=jnp.float32
        )
        all_skeletons = lax.all_gather(
            skeleton.astype(jnp.bfloat16)[None], "blk", axis=0, tiled=True
        )
        selected = all_skeletons[far_local]
        far_sum = jnp.einsum(
            "jck,jkm->cm", selected, coupling_local, preferred_element_type=jnp.float32
        )
        result = result + jnp.einsum(
            "ck,lki->lci",
            far_sum.astype(jnp.bfloat16),
            basis_local,
            preferred_element_type=jnp.float32,
        )
        result = result.at[owner_leaf, :, owner_point].add(far_sum.T)
        applied = (local_noise * direction[0, 0] + result)[None, None]
        curve = lax.psum(column_sum(direction * applied), ("row", "blk"))
        step_size = norm_now / curve
        solution = solution + step_size[:, None] * direction
        residual = residual - step_size[:, None] * applied
        norm_next = residual_sum(residual)
        direction = residual + (norm_next / norm_now)[:, None] * direction
        norm_now = norm_next
    total = lax.psum(column_sum(right_side * solution), ("row", "blk"))
    tracer_count = (
        lax.axis_size("row") * lax.axis_size("blk") * right_side.shape[2] * right_side.shape[4]
    )
    quadratic = total / tracer_count
    return (solution, residual, quadratic)


def solution(mesh):
    return jax.shard_map(
        local,
        mesh=mesh,
        in_specs=(
            P("row", "blk", None, None, None),
            P("row", "blk", None, None),
            P("row", "blk", None, None, None, None),
            P("row", "blk", None, None, None),
            P("row", "blk", None),
            P("row", "blk", None),
            P("row", "blk", None, None, None),
        ),
        out_specs=(P("row", "blk", None, None, None), P("row", "blk", None, None, None), P()),
        check_vma=False,
    )
```

profile of v0, /device:TPU:0, one launch (start us, length us, event | category | flops | bytes accessed | tf_op | source)
XLA Modules:
  0.0 537.6 jit_solution(16591721626279821936)
XLA Ops:
  5.8 30.8 %all-gather = bf16[256,64]{1,0:T(8,128)(2,1)S(1)} all-gather(bf16[32,64]{1,0:T(8,128)(2,1)S(1)} %fusion.12), channel_id=2, replica_groups=mesh['row'=4,'blk'=8] {'blk'}, dimensions={0}, use_global_device_ids=true | all-gather | bytes 36864 | tf_op jit(solution)/shard_map/all_gather | solution.py:70
  37.3 4.2 collective-permute-start.3
  43.5 5.1 collective-permute-done.2
  48.8 5.4 %fusion.95 = f32[2,4,32,256,1]{3,2,4,1,0:T(8,128)S(1)} fusion(bf16[2,4,9,32,256]{4,3,2,1,0:T(8,128)(2,1)S(1)} %fusion.58, bf16[2,4,9,256,256]{4,3,2,1,0:T(8,128)(2,1)} %bitcast.461), kind=kOutput, calls=%fused_computation.214 | convolution fusion | flops 301989888 | bytes 10878976 | tf_op jit(solution)/shard_map/abkci,abkij->abcj/dot_general | solution.py:62
  54.7 3.7 scatter_fusion
  59.0 36.9 %all-reduce = (f32[32]{0:T(128)S(1)}, f32[32]{0:T(128)S(1)}) all-reduce(f32[32]{0:T(128)S(1)} %get-tuple-element.32, f32[32]{0:T(128)S(1)} %fusion.16), channel_id=1, replica_groups=mesh['row'=4,'blk'=8] {'row','blk'}, use_global_device_ids=true, to_apply=%region_1.2 | all-reduce | flops 64 | bytes 512 | tf_op jit(solution)/shard_map/psum | solution.py:43
  96.1 42.0 %psum.65 = f32[32]{0:T(128)S(1)} all-reduce(f32[32]{0:T(128)S(1)} %multiply_reduce_fusion.3), channel_id=1, replica_groups=mesh['row'=4,'blk'=8] {'row','blk'}, use_global_device_ids=true, to_apply=%region_6.7 | all-reduce | flops 32 | bytes 256 | tf_op jit(solution)/shard_map/psum | solution.py:43
  140.2 30.6 %all-gather.1 = bf16[256,64]{1,0:T(8,128)(2,1)S(1)} all-gather(bf16[32,64]{1,0:T(8,128)(2,1)S(1)} %fusion.13), channel_id=3, replica_groups=mesh['row'=4,'blk'=8] {'blk'}, dimensions={0}, use_global_device_ids=true | all-gather | bytes 36864 | tf_op jit(solution)/shard_map/all_gather | solution.py:70
  176.5 5.1 collective-permute-done.6
  181.8 5.4 %fusion.96 = f32[2,4,32,256,1]{3,2,4,1,0:T(8,128)S(1)} fusion(bf16[2,4,9,32,256]{4,3,2,1,0:T(8,128)(2,1)S(1)} %fusion.48, bf16[2,4,9,256,256]{4,3,2,1,0:T(8,128)(2,1)} %bitcast.462), kind=kOutput, calls=%fused_computation.215 | convolution fusion | flops 301989888 | bytes 10878976 | tf_op jit(solution)/shard_map/abkci,abkij->abcj/dot_general | solution.py:62
  191.8 36.9 %psum.66 = f32[32]{0:T(128)S(1)} all-reduce(f32[32]{0:T(128)S(1)} %fusion.19), channel_id=1, replica_groups=mesh['row'=4,'blk'=8] {'row','blk'}, use_global_device_ids=true, to_apply=%region_9.10 | all-reduce | flops 32 | bytes 256 | tf_op jit(solution)/shard_map/psum | solution.py:85
  229.0 41.7 %psum.67 = f32[32]{0:T(128)S(1)} all-reduce(f32[32]{0:T(128)S(1)} %get-tuple-element.13), channel_id=1, replica_groups=mesh['row'=4,'blk'=8] {'row','blk'}, use_global_device_ids=true, to_apply=%region_11.12 | all-reduce | flops 32 | bytes 256 | tf_op jit(solution)/shard_map/psum | solution.py:43
  272.9 30.5 %all-gather.2 = bf16[256,64]{1,0:T(8,128)(2,1)S(1)} all-gather(bf16[32,64]{1,0:T(8,128)(2,1)S(1)} %fusion.14), channel_id=4, replica_groups=mesh['row'=4,'blk'=8] {'blk'}, dimensions={0}, use_global_device_ids=true | all-gather | bytes 36864 | tf_op jit(solution)/shard_map/all_gather | solution.py:70
  309.2 5.1 collective-permute-done.10
  314.5 5.4 %fusion.97 = f32[2,4,32,256,1]{3,2,4,1,0:T(8,128)S(1)} fusion(bf16[2,4,9,32,256]{4,3,2,1,0:T(8,128)(2,1)S(1)} %fusion.38, bf16[2,4,9,256,256]{4,3,2,1,0:T(8,128)(2,1)} %bitcast.463), kind=kOutput, calls=%fused_computation.216 | convolution fusion | flops 301989888 | bytes 10878976 | tf_op jit(solution)/shard_map/abkci,abkij->abcj/dot_general | solution.py:62
  320.4 3.7 scatter_fusion.2
  324.5 36.9 %psum.68 = f32[32]{0:T(128)S(1)} all-reduce(f32[32]{0:T(128)S(1)} %fusion.18), channel_id=1, replica_groups=mesh['row'=4,'blk'=8] {'row','blk'}, use_global_device_ids=true, to_apply=%region_14.15 | all-reduce | flops 32 | bytes 256 | tf_op jit(solution)/shard_map/psum | solution.py:85
  361.6 42.0 %psum.69 = f32[32]{0:T(128)S(1)} all-reduce(f32[32]{0:T(128)S(1)} %get-tuple-element.9), channel_id=1, replica_groups=mesh['row'=4,'blk'=8] {'row','blk'}, use_global_device_ids=true, to_apply=%region_16.17 | all-reduce | flops 32 | bytes 256 | tf_op jit(solution)/shard_map/psum | solution.py:43
  405.7 30.6 %all-gather.3 = bf16[256,64]{1,0:T(8,128)(2,1)S(1)} all-gather(bf16[32,64]{1,0:T(8,128)(2,1)S(1)} %fusion.15), channel_id=5, replica_groups=mesh['row'=4,'blk'=8] {'blk'}, dimensions={0}, use_global_device_ids=true | all-gather | bytes 36864 | tf_op jit(solution)/shard_map/all_gather | solution.py:70
  442.0 5.1 collective-permute-done.14
  447.3 5.4 %fusion.98 = f32[2,4,32,256,1]{3,2,4,1,0:T(8,128)S(1)} fusion(bf16[2,4,9,32,256]{4,3,2,1,0:T(8,128)(2,1)S(1)} %fusion.28, bf16[2,4,9,256,256]{4,3,2,1,0:T(8,128)(2,1)} %bitcast.464), kind=kOutput, calls=%fused_computation.217 | convolution fusion | flops 301989888 | bytes 10878976 | tf_op jit(solution)/shard_map/abkci,abkij->abcj/dot_general | solution.py:62
  453.3 3.7 scatter_fusion.3
  457.4 36.9 %psum.70 = f32[32]{0:T(128)S(1)} all-reduce(f32[32]{0:T(128)S(1)} %fusion.17), channel_id=1, replica_groups=mesh['row'=4,'blk'=8] {'row','blk'}, use_global_device_ids=true, to_apply=%region_19.20 | all-reduce | flops 32 | bytes 256 | tf_op jit(solution)/shard_map/psum | solution.py:85
  495.3 41.7 %psum.71 = f32[32]{0:T(128)S(1)} all-reduce(f32[32]{0:T(128)S(1)} %get-tuple-element.5), channel_id=1, replica_groups=mesh['row'=4,'blk'=8] {'row','blk'}, use_global_device_ids=true, to_apply=%region_21.22 | all-reduce | flops 32 | bytes 256 | tf_op jit(solution)/shard_map/psum | solution.py:92
  (153 shorter events, 41.6 us)
Async XLA Ops:
  0.6 5.0 copy-start
  0.6 4.0 copy-start.4
  0.7 36.0 %copy-start.5 = (s32[1,1,7]{2,1,0:T(1,128)S(1)}, s32[1,1,7]{2,1,0:T(1,128)}, u32[]{:S(2)}) copy-start(s32[1,1,7]{2,1,0:T(1,128)} %param.12) | copy-start | bytes 88
  0.7 40.9 %copy-start.2 = (bf16[1,1,7,64,64]{4,3,2,1,0:T(8,128)(2,1)S(1)}, bf16[1,1,7,64,64]{4,3,2,1,0:T(8,128)(2,1)}, u32[]{:S(2)}) copy-start(bf16[1,1,7,64,64]{4,3,2,1,0:T(8,128)(2,1)} %param.13) | copy-start | bytes 172036
  1.9 39.9 %copy-start.1 = (f32[1,1,8,32,256]{4,3,2,1,0:T(8,128)S(1)}, f32[1,1,8,32,256]{4,3,2,1,0:T(8,128)}, u32[]{:S(2)}) copy-start(f32[1,1,8,32,256]{4,3,2,1,0:T(8,128)} %param.7) | copy-start | bytes 786436
  1.9 35.3 %collective-permute-start.1 = (bf16[1,4,32,256]{3,2,1,0:T(8,128)(2,1)S(1)}, bf16[1,4,32,256]{3,2,1,0:T(8,128)(2,1)S(1)}, u32[]{:S(2)}, u32[]{:S(2)}) collective-permute-start(bf16[1,4,32,256]{3,2,1,0:T(8,128)(2,1)S(1)} %get-tuple-element.45), channel_id=1, source_target_pairs={{8,0},{16,8},{24,16},{0,24},{9,1},{17,9},{25,17},{1,25},{10,2},{18... | collective-permute-start | bytes 196616 | tf_op jit(solution)/shard_map/ppermute | solution.py:19
  4.4 32.9 %collective-permute-start = (bf16[1,4,32,256]{3,2,1,0:T(8,128)(2,1)S(1)}, bf16[1,4,32,256]{3,2,1,0:T(8,128)(2,1)S(1)}, u32[]{:S(2)}, u32[]{:S(2)}) collective-permute-start(bf16[1,4,32,256]{3,2,1,0:T(8,128)(2,1)S(1)} %get-tuple-element.44), channel_id=1, source_target_pairs={{0,8},{8,16},{16,24},{24,0},{1,9},{9,17},{17,25},{25,1},{2,10},{10... | collective-permute-start | bytes 196616 | tf_op jit(solution)/shard_map/ppermute | solution.py:18
  37.3 6.1 %collective-permute-start.3 = (bf16[4,1,32,256]{3,2,1,0:T(8,128)(2,1)S(1)}, bf16[4,1,32,256]{3,2,1,0:T(8,128)(2,1)S(1)}, u32[]{:S(2)}, u32[]{:S(2)}) collective-permute-start(bf16[4,1,32,256]{3,2,1,0:T(8,128)(2,1)S(1)} %get-tuple-element.36), channel_id=1, source_target_pairs={{1,0},{2,1},{3,2},{4,3},{5,4},{6,5},{7,6},{0,7},{9,8},{10,9},{11,1... | collective-permute-start | bytes 196616 | tf_op jit(solution)/shard_map/ppermute | solution.py:19
  41.5 7.0 %collective-permute-start.2 = (bf16[4,1,32,256]{3,2,1,0:T(8,128)(2,1)S(1)}, bf16[4,1,32,256]{3,2,1,0:T(8,128)(2,1)S(1)}, u32[]{:S(2)}, u32[]{:S(2)}) collective-permute-start(bf16[4,1,32,256]{3,2,1,0:T(8,128)(2,1)S(1)} %get-tuple-element.37), channel_id=1, source_target_pairs={{0,1},{1,2},{2,3},{3,4},{4,5},{5,6},{6,7},{7,0},{8,9},{9,10},{10,1... | collective-permute-start | bytes 196616 | tf_op jit(solution)/shard_map/ppermute | solution.py:18
  48.7 5.4 %copy-start.3 = (f32[1,1,8,256]{3,2,1,0:T(8,128)S(1)}, f32[1,1,8,256]{3,2,1,0:T(8,128)}, u32[]{:S(2)}) copy-start(f32[1,1,8,256]{3,2,1,0:T(8,128)} %param.8) | copy-start | bytes 24580
  138.2 33.1 %collective-permute-start.5 = (bf16[1,4,32,256]{3,2,1,0:T(8,128)(2,1)S(1)}, bf16[1,4,32,256]{3,2,1,0:T(8,128)(2,1)S(1)}, u32[]{:S(2)}, u32[]{:S(2)}) collective-permute-start(bf16[1,4,32,256]{3,2,1,0:T(8,128)(2,1)S(1)} %get-tuple-element.43), channel_id=1, source_target_pairs={{8,0},{16,8},{24,16},{0,24},{9,1},{17,9},{25,17},{1,25},{10,2},{18... | collective-permute-start | bytes 196616 | tf_op jit(solution)/shard_map/ppermute | solution.py:19
  138.6 32.7 %collective-permute-start.4 = (bf16[1,4,32,256]{3,2,1,0:T(8,128)(2,1)S(1)}, bf16[1,4,32,256]{3,2,1,0:T(8,128)(2,1)S(1)}, u32[]{:S(2)}, u32[]{:S(2)}) collective-permute-start(bf16[1,4,32,256]{3,2,1,0:T(8,128)(2,1)S(1)} %get-tuple-element.42), channel_id=1, source_target_pairs={{0,8},{8,16},{16,24},{24,0},{1,9},{9,17},{17,25},{25,1},{2,10},{10... | collective-permute-start | bytes 196616 | tf_op jit(solution)/shard_map/ppermute | solution.py:18
  171.4 5.2 collective-permute-start.7
  174.6 7.0 %collective-permute-start.6 = (bf16[4,1,32,256]{3,2,1,0:T(8,128)(2,1)S(1)}, bf16[4,1,32,256]{3,2,1,0:T(8,128)(2,1)S(1)}, u32[]{:S(2)}, u32[]{:S(2)}) collective-permute-start(bf16[4,1,32,256]{3,2,1,0:T(8,128)(2,1)S(1)} %get-tuple-element.31), channel_id=1, source_target_pairs={{0,1},{1,2},{2,3},{3,4},{4,5},{5,6},{6,7},{7,0},{8,9},{9,10},{10,1... | collective-permute-start | bytes 196616 | tf_op jit(solution)/shard_map/ppermute | solution.py:18
  270.8 33.2 %collective-permute-start.9 = (bf16[1,4,32,256]{3,2,1,0:T(8,128)(2,1)S(1)}, bf16[1,4,32,256]{3,2,1,0:T(8,128)(2,1)S(1)}, u32[]{:S(2)}, u32[]{:S(2)}) collective-permute-start(bf16[1,4,32,256]{3,2,1,0:T(8,128)(2,1)S(1)} %get-tuple-element.41), channel_id=1, source_target_pairs={{8,0},{16,8},{24,16},{0,24},{9,1},{17,9},{25,17},{1,25},{10,2},{18... | collective-permute-start | bytes 196616 | tf_op jit(solution)/shard_map/ppermute | solution.py:19
  271.5 32.5 %collective-permute-start.8 = (bf16[1,4,32,256]{3,2,1,0:T(8,128)(2,1)S(1)}, bf16[1,4,32,256]{3,2,1,0:T(8,128)(2,1)S(1)}, u32[]{:S(2)}, u32[]{:S(2)}) collective-permute-start(bf16[1,4,32,256]{3,2,1,0:T(8,128)(2,1)S(1)} %get-tuple-element.40), channel_id=1, source_target_pairs={{0,8},{8,16},{16,24},{24,0},{1,9},{9,17},{17,25},{25,1},{2,10},{10... | collective-permute-start | bytes 196616 | tf_op jit(solution)/shard_map/ppermute | solution.py:18
  304.1 5.1 collective-permute-start.11
  307.3 7.0 %collective-permute-start.10 = (bf16[4,1,32,256]{3,2,1,0:T(8,128)(2,1)S(1)}, bf16[4,1,32,256]{3,2,1,0:T(8,128)(2,1)S(1)}, u32[]{:S(2)}, u32[]{:S(2)}) collective-permute-start(bf16[4,1,32,256]{3,2,1,0:T(8,128)(2,1)S(1)} %get-tuple-element.27), channel_id=1, source_target_pairs={{0,1},{1,2},{2,3},{3,4},{4,5},{5,6},{6,7},{7,0},{8,9},{9,10},{10,1... | collective-permute-start | bytes 196616 | tf_op jit(solution)/shard_map/ppermute | solution.py:18
  403.7 33.1 %collective-permute-start.13 = (bf16[1,4,32,256]{3,2,1,0:T(8,128)(2,1)S(1)}, bf16[1,4,32,256]{3,2,1,0:T(8,128)(2,1)S(1)}, u32[]{:S(2)}, u32[]{:S(2)}) collective-permute-start(bf16[1,4,32,256]{3,2,1,0:T(8,128)(2,1)S(1)} %get-tuple-element.39), channel_id=1, source_target_pairs={{8,0},{16,8},{24,16},{0,24},{9,1},{17,9},{25,17},{1,25},{10,2},{18... | collective-permute-start | bytes 196616 | tf_op jit(solution)/shard_map/ppermute | solution.py:19
  404.1 32.8 %collective-permute-start.12 = (bf16[1,4,32,256]{3,2,1,0:T(8,128)(2,1)S(1)}, bf16[1,4,32,256]{3,2,1,0:T(8,128)(2,1)S(1)}, u32[]{:S(2)}, u32[]{:S(2)}) collective-permute-start(bf16[1,4,32,256]{3,2,1,0:T(8,128)(2,1)S(1)} %get-tuple-element.38), channel_id=1, source_target_pairs={{0,8},{8,16},{16,24},{24,0},{1,9},{9,17},{17,25},{25,1},{2,10},{10... | collective-permute-start | bytes 196616 | tf_op jit(solution)/shard_map/ppermute | solution.py:18
  436.9 5.1 collective-permute-start.15
  440.1 7.0 %collective-permute-start.14 = (bf16[4,1,32,256]{3,2,1,0:T(8,128)(2,1)S(1)}, bf16[4,1,32,256]{3,2,1,0:T(8,128)(2,1)S(1)}, u32[]{:S(2)}, u32[]{:S(2)}) collective-permute-start(bf16[4,1,32,256]{3,2,1,0:T(8,128)(2,1)S(1)} %get-tuple-element.23), channel_id=1, source_target_pairs={{0,1},{1,2},{2,3},{3,4},{4,5},{5,6},{6,7},{7,0},{8,9},{9,10},{10,1... | collective-permute-start | bytes 196616 | tf_op jit(solution)/shard_map/ppermute | solution.py:18
where the time goes:
time: 539 us; the launch traced here: 538 us
  blocking collectives  438 us (81%)
  waiting for transfers between devices  26.4 us (5%)
  matrix products  23.9 us (4%)
  other arithmetic  19.6 us (4%)
  starting transfers between devices  18.2 us (3%)
  local copies, waits for them, and re-layouts  10.6 us (2%)
    psum x4, blocking collectives, residual_sum(): return lax.psum(column_sum(values * values), ('row', 'blk'))  163 us
    all_gather x4, blocking collectives, local(): lax.all_gather(skeleton.astype(jnp.bfloat16)[None], 'blk', axis=0, tiled=...  123 us
    psum x3, blocking collectives, local(): curve = lax.psum(column_sum(direction * applied), ('row', 'blk'))  111 us
    psum x1, blocking collectives, local(): total = lax.psum(column_sum(right_side * solution), ('row', 'blk'))  41.7 us
    dot_general x4, matrix products, local(): jnp.einsum('abkci,abkij->abcj', sources, blocks_grid, preferred_element_t...  21.6 us
    ppermute x8, waiting for transfers between devices, extended_2(): before = lax.ppermute(last, axis, up)  20.2 us
    ppermute x8, starting transfers between devices, extended_2(): after = lax.ppermute(leading, axis, down)  17.8 us
    scatter-add x4, other arithmetic, local(): result = result.at[owner_leaf, :, owner_point].add(far_sum.T)  14.7 us
  transfers between devices with their start and end apart: 16, of which 8 were waited for; matrix products, arithmetic and copies ran while one was open for 2% of the time, Pallas kernels for 0%

commit v1 on v0

--- a/solution.py
+++ b/solution.py
@@ -82,7 +82,7 @@
         )
         result = result.at[owner_leaf, :, owner_point].add(far_sum.T)
         applied = (local_noise * direction[0, 0] + result)[None, None]
-        curve = lax.psum(column_sum(direction * applied), ("row", "blk"))
+        curve = lax.psum(lax.psum(column_sum(direction * applied), "blk"), "row")
         step_size = norm_now / curve
         solution = solution + step_size[:, None] * direction
         residual = residual - step_size[:, None] * applied

time: 539 us -> 505 us (0.937)
  blocking collectives: 438 us -> 407 us
  waiting for transfers between devices: 26.4 us -> 20.1 us
    psum x3 -> x8, blocking collectives: 111 us -> 94.4 us  [local(): curve = lax.psum(lax.psum(column_sum(direction * applied), 'blk'), 'row')]
    psum x4, blocking collectives: 163 us -> 152 us  [residual_sum(): return lax.psum(column_sum(values * values), ('row', 'blk'))]
  transfers between devices with their start and end apart: 16 -> 16, of which waited for: 8 -> 6; matrix products, arithmetic and copies ran while one was open for 2% -> 2% of each run, Pallas kernels for 0% -> 0%
where the time goes in v1:
time: 505 us; the launch traced here: 503 us
  blocking collectives  407 us (81%)
  matrix products  23.9 us (5%)
  starting transfers between devices  20.3 us (4%)
  waiting for transfers between devices  20.1 us (4%)
  other arithmetic  19.6 us (4%)
  local copies, waits for them, and re-layouts  10.6 us (2%)
    psum x4, blocking collectives, residual_sum(): return lax.psum(column_sum(values * values), ('row', 'blk'))  152 us
    all_gather x4, blocking collectives, local(): lax.all_gather(skeleton.astype(jnp.bfloat16)[None], 'blk', axis=0, tiled=...  123 us
    psum x8, blocking collectives, local(): curve = lax.psum(lax.psum(column_sum(direction * applied), 'blk'), 'row')  94.4 us
    psum x1, blocking collectives, local(): total = lax.psum(column_sum(right_side * solution), ('row', 'blk'))  37.8 us
    dot_general x4, matrix products, local(): jnp.einsum('abkci,abkij->abcj', sources, blocks_grid, preferred_element_t...  21.6 us
    ppermute x8, starting transfers between devices, extended_2(): after = lax.ppermute(leading, axis, down)  20 us
    ppermute x8, waiting for transfers between devices, extended_2(): before = lax.ppermute(last, axis, up)  15.2 us
    scatter-add x4, other arithmetic, local(): result = result.at[owner_leaf, :, owner_point].add(far_sum.T)  14.7 us
  transfers between devices with their start and end apart: 16, of which 6 were waited for; matrix products, arithmetic and copies ran while one was open for 2% of the time, Pallas kernels for 0%

profile of v1, /device:TPU:0, one launch (start us, length us, event | category | flops | bytes accessed | tf_op | source)
XLA Modules:
  0.0 503.2 jit_solution(5280373268941284951)
XLA Ops:
  5.8 30.8 %all-gather = bf16[256,64]{1,0:T(8,128)(2,1)S(1)} all-gather(bf16[32,64]{1,0:T(8,128)(2,1)S(1)} %fusion.12), channel_id=2, replica_groups=mesh['row'=4,'blk'=8] {'blk'}, dimensions={0}, use_global_device_ids=true | all-gather | bytes 36864 | tf_op jit(solution)/shard_map/all_gather | solution.py:70
  41.7 39.6 %psum.91 = f32[32]{0:T(128)S(1)} all-reduce(f32[32]{0:T(128)S(1)} %get-tuple-element.30), channel_id=1, replica_groups=mesh['row'=4,'blk'=8] {'row','blk'}, use_global_device_ids=true, to_apply=%region_1.2 | all-reduce | flops 32 | bytes 256 | tf_op jit(solution)/shard_map/psum | solution.py:43
  82.1 5.4 %fusion.95 = f32[2,4,32,256,1]{3,2,4,1,0:T(8,128)S(1)} fusion(bf16[2,4,9,32,256]{4,3,2,1,0:T(8,128)(2,1)S(1)} %fusion.58, bf16[2,4,9,256,256]{4,3,2,1,0:T(8,128)(2,1)} %bitcast.461), kind=kOutput, calls=%fused_computation.214 | convolution fusion | flops 301989888 | bytes 10878976 | tf_op jit(solution)/shard_map/abkci,abkij->abcj/dot_general | solution.py:62
  92.3 20.4 %psum.92 = f32[32]{0:T(128)S(1)} all-reduce(f32[32]{0:T(128)S(1)} %fusion.16), channel_id=1, replica_groups=mesh['row'=4,'blk'=8] {'blk'}, use_global_device_ids=true, to_apply=%region_4.5 | all-reduce | flops 32 | bytes 256 | tf_op jit(solution)/shard_map/psum | solution.py:85
  112.7 5.6 %psum.93 = f32[32]{0:T(128)S(1)} all-reduce(f32[32]{0:T(128)S(1)} %psum.92), channel_id=1, replica_groups=mesh['row'=4,'blk'=8] {'row'}, use_global_device_ids=true, to_apply=%region_5.6 | all-reduce | flops 32 | bytes 256 | tf_op jit(solution)/shard_map/psum | solution.py:85
  118.6 36.9 %psum.94 = f32[32]{0:T(128)S(1)} all-reduce(f32[32]{0:T(128)S(1)} %multiply_reduce_fusion.3), channel_id=1, replica_groups=mesh['row'=4,'blk'=8] {'row','blk'}, use_global_device_ids=true, to_apply=%region_7.8 | all-reduce | flops 32 | bytes 256 | tf_op jit(solution)/shard_map/psum | solution.py:43
  157.6 30.5 %all-gather.1 = bf16[256,64]{1,0:T(8,128)(2,1)S(1)} all-gather(bf16[32,64]{1,0:T(8,128)(2,1)S(1)} %fusion.13), channel_id=3, replica_groups=mesh['row'=4,'blk'=8] {'blk'}, dimensions={0}, use_global_device_ids=true | all-gather | bytes 36864 | tf_op jit(solution)/shard_map/all_gather | solution.py:70
  194.6 5.1 %collective-permute-done.6 = bf16[4,1,32,256]{3,2,1,0:T(8,128)(2,1)S(1)} collective-permute-done((bf16[4,1,32,256]{3,2,1,0:T(8,128)(2,1)S(1)}, bf16[4,1,32,256]{3,2,1,0:T(8,128)(2,1)S(1)}, u32[]{:S(2)}, u32[]{:S(2)}) %collective-permute-start.6) | collective-permute-done | bytes 65568 | tf_op jit(solution)/shard_map/ppermute | solution.py:18
  199.9 5.4 %fusion.96 = f32[2,4,32,256,1]{3,2,4,1,0:T(8,128)S(1)} fusion(bf16[2,4,9,32,256]{4,3,2,1,0:T(8,128)(2,1)S(1)} %fusion.48, bf16[2,4,9,256,256]{4,3,2,1,0:T(8,128)(2,1)} %bitcast.462), kind=kOutput, calls=%fused_computation.215 | convolution fusion | flops 301989888 | bytes 10878976 | tf_op jit(solution)/shard_map/abkci,abkij->abcj/dot_general | solution.py:62
  210.0 17.1 %psum.95 = f32[32]{0:T(128)S(1)} all-reduce(f32[32]{0:T(128)S(1)} %fusion.19), channel_id=1, replica_groups=mesh['row'=4,'blk'=8] {'blk'}, use_global_device_ids=true, to_apply=%region_10.11 | all-reduce | flops 32 | bytes 256 | tf_op jit(solution)/shard_map/psum | solution.py:85
  227.1 5.6 %psum.96 = f32[32]{0:T(128)S(1)} all-reduce(f32[32]{0:T(128)S(1)} %psum.95), channel_id=1, replica_groups=mesh['row'=4,'blk'=8] {'row'}, use_global_device_ids=true, to_apply=%region_11.12 | all-reduce | flops 32 | bytes 256 | tf_op jit(solution)/shard_map/psum | solution.py:85
  233.0 37.8 %psum.97 = f32[32]{0:T(128)S(1)} all-reduce(f32[32]{0:T(128)S(1)} %get-tuple-element.11), channel_id=1, replica_groups=mesh['row'=4,'blk'=8] {'row','blk'}, use_global_device_ids=true, to_apply=%region_13.14 | all-reduce | flops 32 | bytes 256 | tf_op jit(solution)/shard_map/psum | solution.py:43
  273.0 30.7 %all-gather.2 = bf16[256,64]{1,0:T(8,128)(2,1)S(1)} all-gather(bf16[32,64]{1,0:T(8,128)(2,1)S(1)} %fusion.14), channel_id=4, replica_groups=mesh['row'=4,'blk'=8] {'blk'}, dimensions={0}, use_global_device_ids=true | all-gather | bytes 36864 | tf_op jit(solution)/shard_map/all_gather | solution.py:70
  310.2 5.1 %collective-permute-done.10 = bf16[4,1,32,256]{3,2,1,0:T(8,128)(2,1)S(1)} collective-permute-done((bf16[4,1,32,256]{3,2,1,0:T(8,128)(2,1)S(1)}, bf16[4,1,32,256]{3,2,1,0:T(8,128)(2,1)S(1)}, u32[]{:S(2)}, u32[]{:S(2)}) %collective-permute-start.10) | collective-permute-done | bytes 65568 | tf_op jit(solution)/shard_map/ppermute | solution.py:18
  315.5 5.4 %fusion.97 = f32[2,4,32,256,1]{3,2,4,1,0:T(8,128)S(1)} fusion(bf16[2,4,9,32,256]{4,3,2,1,0:T(8,128)(2,1)S(1)} %fusion.38, bf16[2,4,9,256,256]{4,3,2,1,0:T(8,128)(2,1)} %bitcast.463), kind=kOutput, calls=%fused_computation.216 | convolution fusion | flops 301989888 | bytes 10878976 | tf_op jit(solution)/shard_map/abkci,abkij->abcj/dot_general | solution.py:62
  325.5 17.1 %psum.98 = f32[32]{0:T(128)S(1)} all-reduce(f32[32]{0:T(128)S(1)} %fusion.18), channel_id=1, replica_groups=mesh['row'=4,'blk'=8] {'blk'}, use_global_device_ids=true, to_apply=%region_16.17 | all-reduce | flops 32 | bytes 256 | tf_op jit(solution)/shard_map/psum | solution.py:85
  342.6 5.6 %psum.99 = f32[32]{0:T(128)S(1)} all-reduce(f32[32]{0:T(128)S(1)} %psum.98), channel_id=1, replica_groups=mesh['row'=4,'blk'=8] {'row'}, use_global_device_ids=true, to_apply=%region_17.18 | all-reduce | flops 32 | bytes 256 | tf_op jit(solution)/shard_map/psum | solution.py:85
  348.5 38.0 %psum.100 = f32[32]{0:T(128)S(1)} all-reduce(f32[32]{0:T(128)S(1)} %get-tuple-element.7), channel_id=1, replica_groups=mesh['row'=4,'blk'=8] {'row','blk'}, use_global_device_ids=true, to_apply=%region_19.20 | all-reduce | flops 32 | bytes 256 | tf_op jit(solution)/shard_map/psum | solution.py:43
  388.6 30.5 %all-gather.3 = bf16[256,64]{1,0:T(8,128)(2,1)S(1)} all-gather(bf16[32,64]{1,0:T(8,128)(2,1)S(1)} %fusion.15), channel_id=5, replica_groups=mesh['row'=4,'blk'=8] {'blk'}, dimensions={0}, use_global_device_ids=true | all-gather | bytes 36864 | tf_op jit(solution)/shard_map/all_gather | solution.py:70
  425.7 5.1 %collective-permute-done.14 = bf16[4,1,32,256]{3,2,1,0:T(8,128)(2,1)S(1)} collective-permute-done((bf16[4,1,32,256]{3,2,1,0:T(8,128)(2,1)S(1)}, bf16[4,1,32,256]{3,2,1,0:T(8,128)(2,1)S(1)}, u32[]{:S(2)}, u32[]{:S(2)}) %collective-permute-start.14) | collective-permute-done | bytes 65568 | tf_op jit(solution)/shard_map/ppermute | solution.py:18
  430.9 5.4 %fusion.98 = f32[2,4,32,256,1]{3,2,4,1,0:T(8,128)S(1)} fusion(bf16[2,4,9,32,256]{4,3,2,1,0:T(8,128)(2,1)S(1)} %fusion.28, bf16[2,4,9,256,256]{4,3,2,1,0:T(8,128)(2,1)} %bitcast.464), kind=kOutput, calls=%fused_computation.217 | convolution fusion | flops 301989888 | bytes 10878976 | tf_op jit(solution)/shard_map/abkci,abkij->abcj/dot_general | solution.py:62
  441.0 17.1 %psum.101 = f32[32]{0:T(128)S(1)} all-reduce(f32[32]{0:T(128)S(1)} %fusion.17), channel_id=1, replica_groups=mesh['row'=4,'blk'=8] {'blk'}, use_global_device_ids=true, to_apply=%region_22.23 | all-reduce | flops 32 | bytes 256 | tf_op jit(solution)/shard_map/psum | solution.py:85
  458.1 5.6 %psum.102 = f32[32]{0:T(128)S(1)} all-reduce(f32[32]{0:T(128)S(1)} %psum.101), channel_id=1, replica_groups=mesh['row'=4,'blk'=8] {'row'}, use_global_device_ids=true, to_apply=%region_23.24 | all-reduce | flops 32 | bytes 256 | tf_op jit(solution)/shard_map/psum | solution.py:85
  464.8 37.8 %psum.103 = f32[32]{0:T(128)S(1)} all-reduce(f32[32]{0:T(128)S(1)} %get-tuple-element.3), channel_id=1, replica_groups=mesh['row'=4,'blk'=8] {'row','blk'}, use_global_device_ids=true, to_apply=%region_25.26 | all-reduce | flops 32 | bytes 256 | tf_op jit(solution)/shard_map/psum | solution.py:92
  (158 shorter events, 57.7 us)
Async XLA Ops:
  0.6 5.0 copy-start
  0.6 4.0 copy-start.4
  0.7 36.0 %copy-start.5 = (s32[1,1,7]{2,1,0:T(1,128)S(1)}, s32[1,1,7]{2,1,0:T(1,128)}, u32[]{:S(2)}) copy-start(s32[1,1,7]{2,1,0:T(1,128)} %param.12) | copy-start | bytes 88
  0.7 40.9 %copy-start.2 = (bf16[1,1,7,64,64]{4,3,2,1,0:T(8,128)(2,1)S(1)}, bf16[1,1,7,64,64]{4,3,2,1,0:T(8,128)(2,1)}, u32[]{:S(2)}) copy-start(bf16[1,1,7,64,64]{4,3,2,1,0:T(8,128)(2,1)} %param.13) | copy-start | bytes 172036
  1.9 79.5 %copy-start.1 = (f32[1,1,8,32,256]{4,3,2,1,0:T(8,128)S(1)}, f32[1,1,8,32,256]{4,3,2,1,0:T(8,128)}, u32[]{:S(2)}) copy-start(f32[1,1,8,32,256]{4,3,2,1,0:T(8,128)} %param.7) | copy-start | bytes 786436
  1.9 35.3 %collective-permute-start.1 = (bf16[1,4,32,256]{3,2,1,0:T(8,128)(2,1)S(1)}, bf16[1,4,32,256]{3,2,1,0:T(8,128)(2,1)S(1)}, u32[]{:S(2)}, u32[]{:S(2)}) collective-permute-start(bf16[1,4,32,256]{3,2,1,0:T(8,128)(2,1)S(1)} %get-tuple-element.43), channel_id=1, source_target_pairs={{8,0},{16,8},{24,16},{0,24},{9,1},{17,9},{25,17},{1,25},{10,2},{18... | collective-permute-start | bytes 196616 | tf_op jit(solution)/shard_map/ppermute | solution.py:19
  4.4 32.9 %collective-permute-start = (bf16[1,4,32,256]{3,2,1,0:T(8,128)(2,1)S(1)}, bf16[1,4,32,256]{3,2,1,0:T(8,128)(2,1)S(1)}, u32[]{:S(2)}, u32[]{:S(2)}) collective-permute-start(bf16[1,4,32,256]{3,2,1,0:T(8,128)(2,1)S(1)} %get-tuple-element.42), channel_id=1, source_target_pairs={{0,8},{8,16},{16,24},{24,0},{1,9},{9,17},{17,25},{25,1},{2,10},{10... | collective-permute-start | bytes 196616 | tf_op jit(solution)/shard_map/ppermute | solution.py:18
  37.3 44.5 %collective-permute-start.3 = (bf16[4,1,32,256]{3,2,1,0:T(8,128)(2,1)S(1)}, bf16[4,1,32,256]{3,2,1,0:T(8,128)(2,1)S(1)}, u32[]{:S(2)}, u32[]{:S(2)}) collective-permute-start(bf16[4,1,32,256]{3,2,1,0:T(8,128)(2,1)S(1)} %get-tuple-element.34), channel_id=1, source_target_pairs={{1,0},{2,1},{3,2},{4,3},{5,4},{6,5},{7,6},{0,7},{9,8},{10,9},{11,1... | collective-permute-start | bytes 196616 | tf_op jit(solution)/shard_map/ppermute | solution.py:19
  41.5 40.3 %collective-permute-start.2 = (bf16[4,1,32,256]{3,2,1,0:T(8,128)(2,1)S(1)}, bf16[4,1,32,256]{3,2,1,0:T(8,128)(2,1)S(1)}, u32[]{:S(2)}, u32[]{:S(2)}) collective-permute-start(bf16[4,1,32,256]{3,2,1,0:T(8,128)(2,1)S(1)} %get-tuple-element.35), channel_id=1, source_target_pairs={{0,1},{1,2},{2,3},{3,4},{4,5},{5,6},{6,7},{7,0},{8,9},{9,10},{10,1... | collective-permute-start | bytes 196616 | tf_op jit(solution)/shard_map/ppermute | solution.py:18
  82.1 5.4 %copy-start.3 = (f32[1,1,8,256]{3,2,1,0:T(8,128)S(1)}, f32[1,1,8,256]{3,2,1,0:T(8,128)}, u32[]{:S(2)}) copy-start(f32[1,1,8,256]{3,2,1,0:T(8,128)} %param.8) | copy-start | bytes 24580
  155.6 33.1 %collective-permute-start.5 = (bf16[1,4,32,256]{3,2,1,0:T(8,128)(2,1)S(1)}, bf16[1,4,32,256]{3,2,1,0:T(8,128)(2,1)S(1)}, u32[]{:S(2)}, u32[]{:S(2)}) collective-permute-start(bf16[1,4,32,256]{3,2,1,0:T(8,128)(2,1)S(1)} %get-tuple-element.41), channel_id=1, source_target_pairs={{8,0},{16,8},{24,16},{0,24},{9,1},{17,9},{25,17},{1,25},{10,2},{18... | collective-permute-start | bytes 196616 | tf_op jit(solution)/shard_map/ppermute | solution.py:19
  156.1 32.7 %collective-permute-start.4 = (bf16[1,4,32,256]{3,2,1,0:T(8,128)(2,1)S(1)}, bf16[1,4,32,256]{3,2,1,0:T(8,128)(2,1)S(1)}, u32[]{:S(2)}, u32[]{:S(2)}) collective-permute-start(bf16[1,4,32,256]{3,2,1,0:T(8,128)(2,1)S(1)} %get-tuple-element.40), channel_id=1, source_target_pairs={{0,8},{8,16},{16,24},{24,0},{1,9},{9,17},{17,25},{25,1},{2,10},{10... | collective-permute-start | bytes 196616 | tf_op jit(solution)/shard_map/ppermute | solution.py:18
  188.8 5.9 %collective-permute-start.7 = (bf16[4,1,32,256]{3,2,1,0:T(8,128)(2,1)S(1)}, bf16[4,1,32,256]{3,2,1,0:T(8,128)(2,1)S(1)}, u32[]{:S(2)}, u32[]{:S(2)}) collective-permute-start(bf16[4,1,32,256]{3,2,1,0:T(8,128)(2,1)S(1)} %get-tuple-element.28), channel_id=1, source_target_pairs={{1,0},{2,1},{3,2},{4,3},{5,4},{6,5},{7,6},{0,7},{9,8},{10,9},{11,1... | collective-permute-start | bytes 196616 | tf_op jit(solution)/shard_map/ppermute | solution.py:19
  192.7 7.0 %collective-permute-start.6 = (bf16[4,1,32,256]{3,2,1,0:T(8,128)(2,1)S(1)}, bf16[4,1,32,256]{3,2,1,0:T(8,128)(2,1)S(1)}, u32[]{:S(2)}, u32[]{:S(2)}) collective-permute-start(bf16[4,1,32,256]{3,2,1,0:T(8,128)(2,1)S(1)} %get-tuple-element.29), channel_id=1, source_target_pairs={{0,1},{1,2},{2,3},{3,4},{4,5},{5,6},{6,7},{7,0},{8,9},{9,10},{10,1... | collective-permute-start | bytes 196616 | tf_op jit(solution)/shard_map/ppermute | solution.py:18
  271.0 33.3 %collective-permute-start.9 = (bf16[1,4,32,256]{3,2,1,0:T(8,128)(2,1)S(1)}, bf16[1,4,32,256]{3,2,1,0:T(8,128)(2,1)S(1)}, u32[]{:S(2)}, u32[]{:S(2)}) collective-permute-start(bf16[1,4,32,256]{3,2,1,0:T(8,128)(2,1)S(1)} %get-tuple-element.39), channel_id=1, source_target_pairs={{8,0},{16,8},{24,16},{0,24},{9,1},{17,9},{25,17},{1,25},{10,2},{18... | collective-permute-start | bytes 196616 | tf_op jit(solution)/shard_map/ppermute | solution.py:19
  271.6 32.7 %collective-permute-start.8 = (bf16[1,4,32,256]{3,2,1,0:T(8,128)(2,1)S(1)}, bf16[1,4,32,256]{3,2,1,0:T(8,128)(2,1)S(1)}, u32[]{:S(2)}, u32[]{:S(2)}) collective-permute-start(bf16[1,4,32,256]{3,2,1,0:T(8,128)(2,1)S(1)} %get-tuple-element.38), channel_id=1, source_target_pairs={{0,8},{8,16},{16,24},{24,0},{1,9},{9,17},{17,25},{25,1},{2,10},{10... | collective-permute-start | bytes 196616 | tf_op jit(solution)/shard_map/ppermute | solution.py:18
  304.3 5.9 %collective-permute-start.11 = (bf16[4,1,32,256]{3,2,1,0:T(8,128)(2,1)S(1)}, bf16[4,1,32,256]{3,2,1,0:T(8,128)(2,1)S(1)}, u32[]{:S(2)}, u32[]{:S(2)}) collective-permute-start(bf16[4,1,32,256]{3,2,1,0:T(8,128)(2,1)S(1)} %get-tuple-element.24), channel_id=1, source_target_pairs={{1,0},{2,1},{3,2},{4,3},{5,4},{6,5},{7,6},{0,7},{9,8},{10,9},{11,1... | collective-permute-start | bytes 196616 | tf_op jit(solution)/shard_map/ppermute | solution.py:19
  308.3 7.0 %collective-permute-start.10 = (bf16[4,1,32,256]{3,2,1,0:T(8,128)(2,1)S(1)}, bf16[4,1,32,256]{3,2,1,0:T(8,128)(2,1)S(1)}, u32[]{:S(2)}, u32[]{:S(2)}) collective-permute-start(bf16[4,1,32,256]{3,2,1,0:T(8,128)(2,1)S(1)} %get-tuple-element.25), channel_id=1, source_target_pairs={{0,1},{1,2},{2,3},{3,4},{4,5},{5,6},{6,7},{7,0},{8,9},{9,10},{10,1... | collective-permute-start | bytes 196616 | tf_op jit(solution)/shard_map/ppermute | solution.py:18
  386.6 33.1 %collective-permute-start.13 = (bf16[1,4,32,256]{3,2,1,0:T(8,128)(2,1)S(1)}, bf16[1,4,32,256]{3,2,1,0:T(8,128)(2,1)S(1)}, u32[]{:S(2)}, u32[]{:S(2)}) collective-permute-start(bf16[1,4,32,256]{3,2,1,0:T(8,128)(2,1)S(1)} %get-tuple-element.37), channel_id=1, source_target_pairs={{8,0},{16,8},{24,16},{0,24},{9,1},{17,9},{25,17},{1,25},{10,2},{18... | collective-permute-start | bytes 196616 | tf_op jit(solution)/shard_map/ppermute | solution.py:19
  387.1 32.7 %collective-permute-start.12 = (bf16[1,4,32,256]{3,2,1,0:T(8,128)(2,1)S(1)}, bf16[1,4,32,256]{3,2,1,0:T(8,128)(2,1)S(1)}, u32[]{:S(2)}, u32[]{:S(2)}) collective-permute-start(bf16[1,4,32,256]{3,2,1,0:T(8,128)(2,1)S(1)} %get-tuple-element.36), channel_id=1, source_target_pairs={{0,8},{8,16},{16,24},{24,0},{1,9},{9,17},{17,25},{25,1},{2,10},{10... | collective-permute-start | bytes 196616 | tf_op jit(solution)/shard_map/ppermute | solution.py:18
  419.8 5.9 %collective-permute-start.15 = (bf16[4,1,32,256]{3,2,1,0:T(8,128)(2,1)S(1)}, bf16[4,1,32,256]{3,2,1,0:T(8,128)(2,1)S(1)}, u32[]{:S(2)}, u32[]{:S(2)}) collective-permute-start(bf16[4,1,32,256]{3,2,1,0:T(8,128)(2,1)S(1)} %get-tuple-element.20), channel_id=1, source_target_pairs={{1,0},{2,1},{3,2},{4,3},{5,4},{6,5},{7,6},{0,7},{9,8},{10,9},{11,1... | collective-permute-start | bytes 196616 | tf_op jit(solution)/shard_map/ppermute | solution.py:19
  423.7 7.0 %collective-permute-start.14 = (bf16[4,1,32,256]{3,2,1,0:T(8,128)(2,1)S(1)}, bf16[4,1,32,256]{3,2,1,0:T(8,128)(2,1)S(1)}, u32[]{:S(2)}, u32[]{:S(2)}) collective-permute-start(bf16[4,1,32,256]{3,2,1,0:T(8,128)(2,1)S(1)} %get-tuple-element.21), channel_id=1, source_target_pairs={{0,1},{1,2},{2,3},{3,4},{4,5},{5,6},{6,7},{7,0},{8,9},{9,10},{10,1... | collective-permute-start | bytes 196616 | tf_op jit(solution)/shard_map/ppermute | solution.py:18
